TPU v7x, 512 devices: a whole 4x8x8 slice. The times are simulated.
512 devices in a mesh: row: 16 (over y, core), col: 32 (over z, x).
Axes of the slice: x: 4, y: 8, z: 8, core: 2. Of those that a mesh axis runs over, the one named last changes fastest.
Arguments:
- row_points: bfloat16 [64, 4096], P(None, 'row'), may hold values from -6 to 6
- col_points: bfloat16 [64, 262144], P(None, 'col'), may hold values from -6 to 6
- random_panel: bfloat16 [262144, 128], P('col'), may hold values from -6 to 6
Outputs:
- left_basis: float32 [4096, 128], P('row')
- coefficients: bfloat16 [128, 262144], P('row', 'col')
All inputs are finite; a program needn't handle non-finite values.
Results may differ from a plain program's by a relative error of at most 0.015.
Values may be sent and summed in bfloat16 or wider, within the bound.
A program may use at most 64 MiB of HBM per device.

v0:
```python
import math

import jax
import jax.numpy as jnp
from jax import lax
from jax.sharding import PartitionSpec as P


def kernel_tile(points_left, left_sq, col_block, exp_scale):
    cross = jnp.einsum("kr,kc->rc", points_left, col_block, preferred_element_type=jnp.float32)
    col_sq = jnp.sum(jnp.square(col_block.astype(jnp.float32)), axis=0)
    return jnp.exp((2.0 * cross - left_sq[:, None] - col_sq[None, :]) * exp_scale)


def per_device(row_points, col_points, random_panel):
    feature_dim, row_dev = row_points.shape
    col_dev, sketch_width = random_panel.shape
    exp_scale = 2.0 / feature_dim
    row_sq = jnp.sum(jnp.square(row_points.astype(jnp.float32)), axis=0)
    block_width = math.gcd(col_dev, 2048)
    block_count = col_dev // block_width
    blocks = col_points.reshape(feature_dim, block_count, block_width).transpose(1, 0, 2)
    panel_blocks = random_panel.reshape(block_count, block_width, sketch_width)
    start_sum = jnp.zeros((row_dev, sketch_width), jnp.float32)

    def add_keep(accum_sum, block_pair):
        kernel = kernel_tile(row_points, row_sq, block_pair[0], exp_scale).astype(jnp.bfloat16)
        return (
            accum_sum + jnp.dot(kernel, block_pair[1], preferred_element_type=jnp.float32),
            kernel,
        )

    partial_value, kernels = lax.scan(add_keep, start_sum, (blocks, panel_blocks))
    sketch = lax.psum(partial_value, "col")
    local_gram = jnp.dot(
        sketch.T, sketch, precision=lax.Precision.HIGHEST, preferred_element_type=jnp.float32
    )
    gram_matrix = lax.psum(local_gram, "row")
    factor = jnp.linalg.cholesky(gram_matrix)
    orthonormal = jax.scipy.linalg.solve_triangular(factor, sketch.T, lower=True).T
    left_basis = orthonormal * math.sqrt(row_dev * lax.axis_size("row"))
    orth_bf = orthonormal.astype(jnp.bfloat16)
    all_terms = jnp.einsum("rq,nrc->qnc", orth_bf, kernels, preferred_element_type=jnp.float32)
    all_terms = all_terms.reshape(sketch_width, col_dev)
    coefficients = lax.psum_scatter(
        all_terms.astype(jnp.bfloat16), "row", scatter_dimension=0, tiled=True
    )
    return (left_basis, coefficients)


def solution(mesh):
    placed = (P(None, "row"), P(None, "col"), P("col", None))
    return jax.shard_map(
        per_device,
        mesh=mesh,
        in_specs=placed,
        out_specs=(P("row", None), P("row", "col")),
        check_vma=False,
    )
```

profile of v0, /device:TPU:1, one launch (start us, length us, event | category | flops | bytes accessed | tf_op | source)
XLA Modules:
  0.0 393.4 jit_solution(6189894932676397929)
XLA Ops:
  7.2 1.9 reshape.24
  9.7 13.3 %while.13 = (s32[]{:T(128)}, f32[256,128]{1,0:T(8,128)S(1)}, bf16[4,256,2048]{1,2,0:T(8,128)(2,1)}, bf16[4,64,2048]{2,1,0:T(8,128)(2,1)S(1)}, bf16[64,256]{1,0:T...) while((s32[]{:T(128)}, f32[256,128]{1,0:T(8,128)S(1)}, ...), condition=%wide.region_3.4_spmd.clone, body=%wide.region_1.3_spmd.clone.sunk | while | flops 204404736 | bytes 4508267 | solution.py:33
  9.8 1.7 bitcast_dynamic-update-slice_fusion.2
  11.5 1.5 convolution_add_fusion.2
  13.1 1.7 bitcast_dynamic-update-slice_fusion.2
  14.9 1.5 convolution_add_fusion.2
  16.5 1.7 bitcast_dynamic-update-slice_fusion.2
  18.2 1.5 convolution_add_fusion.2
  19.8 1.7 bitcast_dynamic-update-slice_fusion.2
  21.5 1.5 convolution_add_fusion.2
  23.1 0.6 copy-done
  23.8 155.1 %all-reduce.3.cloned.1.call-done = f32[256,128]{1,0:T(8,128)} async-done(((f32[256,128]{1,0:T(8,128)}), f32[256,128]{1,0:T(8,128)}) %all-reduce.3.cloned.1.call-update) | async-done | bytes 131088 | tf_op jit(solution)/shard_map/psum | solution.py:34
  178.9 2.0 fusion.17
  181.0 109.8 %all-reduce.5.cloned.1.call-done = f32[128,128]{0,1:T(8,128)} async-done(((f32[128,128]{0,1:T(8,128)}), f32[128,128]{0,1:T(8,128)}) %all-reduce.5.cloned.1.call-update) | async-done | bytes 65552 | tf_op jit(solution)/shard_map/psum | solution.py:38
  290.7 0.9 copy.18
  291.7 0.9 fusion.15
  292.5 11.7 %cholesky.16 = f32[128,128]{1,0:T(8,128)S(1)} custom-call(f32[128,128]{1,0:T(8,128)S(1)} %fusion.15), custom_call_target="Cholesky" | custom-call | tf_op jit(solution)/shard_map/jit(cholesky)/cholesky | solution.py:39
  304.9 0.7 fusion.11
  305.6 9.8 %custom-call.7 = f32[1,128,128]{1,2,0:T(8,128)S(1)} custom-call(f32[1,128,128]{2,1,0:T(8,128)S(1)} %fusion.11), custom_call_target="InvertDiagBlocksLowerTriangular" | custom-call | tf_op jit(solution)/shard_map/jit(_solve_triangular)/triangular_solve | solution.py:40
  315.4 1.8 broadcast_multiply_fusion
  317.2 3.7 convolution_convert_fusion
  320.9 2.5 copy.21
  323.5 4.1 %copy.27 = bf16[128,8192]{1,0:T(8,128)(2,1)} copy(bf16[128,8192]{0,1:T(8,128)(2,1)} %bitcast.49) | data formatting | bytes 4194304
  327.6 59.3 %reduce-scatter.4.cloned.1.call-done = bf16[8,8192]{1,0:T(8,128)(2,1)} async-done(((bf16[128,8192]{1,0:T(8,128)(2,1)}), bf16[8,8192]{1,0:T(8,128)(2,1)}) %reduce-scatter.4.cloned.1.call-update) | async-done | bytes 131088
  (19 shorter events, 1.8 us)
Async XLA Ops:
  7.2 171.7 %all-reduce.3.cloned.1.call-start = ((), (), s32[]{:S(2)}) async-start(), calls=%async_computation.1 | async-start | bytes 262144 | tf_op jit(solution)/shard_map/psum | solution.py:34
  7.2 2.5 copy-start.1
  23.1 0.7 copy-start
  23.7 267.0 %all-reduce.5.cloned.1.call-start = ((), (), s32[]{:S(2)}) async-start(), calls=%async_computation.2 | async-start | bytes 131072 | tf_op jit(solution)/shard_map/psum | solution.py:38
  180.9 205.9 %reduce-scatter.4.cloned.1.call-start = ((), (), s32[]{:S(2)}) async-start(), calls=%async_computation.3 | async-start | bytes 2228224
Sparse Core Ops, SparseCore 0:
  23.9 155.0 all-reduce.2
  181.8 108.8 all-reduce.4
  327.7 59.1 reduce-scatter.3
where the time goes:
time: 395 us; the launch traced here: 393 us
  waiting for transfers between devices  324 us (82%)
  other arithmetic  24 us (6%)
  matrix products  20.4 us (5%)
  between operations  13.8 us (3%)
  local copies, waits for them, and re-layouts  10.6 us (3%)
    psum x1, waiting for transfers between devices, per_device(): sketch = lax.psum(partial_value, 'col')  155 us
    psum x1, waiting for transfers between devices, per_device(): gram_matrix = lax.psum(local_gram, 'row')  110 us
    unnamed x4, waiting for transfers between devices  59.4 us
    another operation x3, other arithmetic, per_device(): factor = jnp.linalg.cholesky(gram_matrix)  12.4 us
    another operation x2, other arithmetic, per_device(): jax.scipy.linalg.solve_triangular(factor, sketch.T, lower=True)  10.5 us
  transfers between devices with their start and end apart: 3, of which 3 were waited for; matrix products, arithmetic and copies ran while one was open for 0% of the time, Pallas kernels for 0%

commit v1 on v0

v1 whole, which is shorter than its diff:
```python
import functools
import math

import jax
import jax.numpy as jnp
from jax import lax
from jax.experimental import pallas as pl
from jax.experimental.pallas import tpu as pltpu
from jax.sharding import PartitionSpec as P

MESH = pl.DeviceIdType.MESH
F32 = jnp.float32
BF16 = jnp.bfloat16
HIGH = lax.Precision.HIGHEST
STAGES = 11
RS, AGC, SY, SZ, SX, RPY, TX, GRS, GAG, SZF, SXF = range(STAGES)
A2A = STAGES
DEPTH = 128


def dot(a, b, ca, cb, precision=None):
    return lax.dot_general(
        a, b, (((ca,), (cb,)), ((), ())), precision=precision, preferred_element_type=F32
    )


def ring(n):
    return sorted(range(n), key=lambda k: -min(k, n - k))


def plane(a, b):
    far = lambda k, n: min(k, n - k)
    both = [(i, j) for i in range(a) for j in range(b) if i or j]
    return sorted(both, key=lambda o: -(far(o[0], a) + far(o[1], b)))


def split3(v):
    hi = v.astype(BF16).astype(F32)
    mid = (v - hi).astype(BF16).astype(F32)
    return hi, mid, v - hi - mid


def split2(v):
    hi = v.astype(BF16)
    return hi, (v - hi.astype(F32)).astype(BF16)


def inverse_factor(gram, block=32, inner=16):
    n = gram.shape[0]
    count, tiles = n // block, block // 8
    lane = lax.broadcasted_iota(jnp.int32, (8, n), 1)
    sub = lax.broadcasted_iota(jnp.int32, (8, n), 0)
    rows = [gram[8 * t : 8 * t + 8] for t in range(n // 8)]
    for b in range(count):
        base = b * block
        p = rows[b * tiles : (b + 1) * tiles]
        col = [None] * block
        diag = [None] * tiles
        for i in range(block):
            ti, si = i // 8, i % 8
            at = lane == base + i
            stop = (i // inner + 1) * inner
            if i % inner == 0:
                for j in range(i, stop):
                    k = base + j
                    col[j] = [
                        jnp.broadcast_to(p[t][:, k : k + 1], (8, n)) if t >= j // 8 else None
                        for t in range(tiles)
                    ]
            d = jnp.broadcast_to(col[i][ti][si : si + 1], (8, n))
            diag[ti] = d if diag[ti] is None else jnp.where(sub == si, d, diag[ti])
            inv = 1.0 / d
            m = [None] * tiles
            for t in range(ti, tiles):
                m[t] = col[i][t] * inv
            m[ti] = jnp.where(sub > si, m[ti], 0.0)
            for j in range(i + 1, stop):
                e = jnp.broadcast_to(col[i][j // 8][j % 8 : j % 8 + 1], (8, n))
                for t in range(j // 8, tiles):
                    col[j][t] = col[j][t] - m[t] * e
            row = jnp.where(at, 1.0, jnp.broadcast_to(p[ti][si : si + 1], (8, n)))
            for t in range(ti, tiles):
                keep = (sub == si).astype(F32) if t == ti else 0.0
                p[t] = jnp.where(at, keep, p[t]) - m[t] * row
        for t in range(tiles):
            dead = (lane > sub + (base + 8 * t)) & (lane < base + block)
            p[t] = jnp.where(dead, 0.0, p[t] * lax.rsqrt(diag[t]))
            rows[b * tiles + t] = p[t]
        if b + 1 < count:
            panel = jnp.concatenate(p, axis=0)
            turned = panel.T
            inside = (lane >= base) & (lane < base + block)
            for u in range(b + 1, count):
                upd = dot(turned[u * block : (u + 1) * block], panel, 1, 0, HIGH)
                for t in range(tiles):
                    at = u * tiles + t
                    rows[at] = jnp.where(inside, 0.0, rows[at]) - upd[8 * t : 8 * t + 8]
    rows = [jnp.where(lane > sub + 8 * t, 0.0, rows[t]) for t in range(n // 8)]
    return jnp.concatenate(rows, axis=0)


def body(
    nrow, ncol, nx, chunk,
    rp_hbm, col_hbm, panel_hbm, left_ref, coef_ref,
    rp, caug, panel, part, rs_buf, srow, sy, sg, rpb, rpt, k2, gpart, grs, gfull, tsum, ts, tr,
    cs, cr,
    send, recv, in_sem,
):
    dim, rows = rp.shape
    cols, rank = panel.shape
    nz, ny = ncol // nx, nrow // 2
    ch = rows // ncol
    gch = rank // nrow
    own_cols = cols // nrow
    chunks = cols // chunk
    scale = 4.0 / dim
    r, c = lax.axis_index("row"), lax.axis_index("col")
    y, core = r // 2, lax.rem(r, 2)
    z, x = c // nx, lax.rem(c, nx)
    partner = y * 2 + 1 - core

    def load(j):
        at = pl.ds(pl.multiple_of(j * chunk, chunk), chunk)
        return (
            pltpu.make_async_copy(col_hbm.at[:, at], caug.at[pl.ds(0, dim), at], in_sem.at[0, j]),
            pltpu.make_async_copy(panel_hbm.at[at, :], panel.at[at, :], in_sem.at[1, j]),
        )

    def put(stage, src, dst, row, col):
        pltpu.make_async_remote_copy(
            src_ref=src, dst_ref=dst, send_sem=send.at[stage], recv_sem=recv.at[stage],
            device_id=(row, col), device_id_type=MESH,
        ).start()

    def landed(stage, ref):
        pltpu.make_async_copy(ref, ref, recv.at[stage]).wait()

    def left_us(stage, ref):
        pltpu.make_async_copy(ref, ref, send.at[stage]).wait()

    def col_at(dz, dx):
        return lax.rem(z + dz, nz) * nx + lax.rem(x + dx, nx)

    def row_at(dy, dc):
        return lax.rem(y + dy, ny) * 2 + (1 - core if dc else core)

    near_z = [k for k in ring(nz) if 0 < min(k, nz - k) <= max(1, nz // 4)]
    far_z = [k for k in ring(nz) if min(k, nz - k) > max(1, nz // 4)]

    def stage_z(k):
        return SZ if k in near_z else SZF

    barrier = pltpu.get_barrier_semaphore()

    for dz, dx in plane(nz, nx):
        to = (r, col_at(dz, dx))
        pl.semaphore_signal(barrier, inc=1, device_id=to, device_id_type=MESH)
    for dy, dc in plane(ny, 2):
        to = (row_at(dy, dc), c)
        pl.semaphore_signal(barrier, inc=1, device_id=to, device_id_type=MESH)

    first = pltpu.make_async_copy(rp_hbm, rp, in_sem.at[0, chunks])
    first.start()
    for j in range(chunks):
        for copy in load(j):
            copy.start()

    def aug_rows(points):
        p = points.astype(F32)
        n = p.shape[1]
        hi, mid, lo = split3(-0.5 * jnp.sum(p * p, axis=0, keepdims=True))
        i = lax.broadcasted_iota(jnp.int32, (DEPTH - dim, n), 0)
        extra = jnp.where(i == 0, hi, jnp.where(i == 1, mid, jnp.where(i == 2, lo, 0.0)))
        extra = jnp.where((i > 2) & (i < 6), 1.0, extra)
        return jnp.concatenate([p, extra], axis=0).T

    first.wait()
    lhs = aug_rows(rp[...]).astype(BF16)
    step = min(256, chunk)

    @pl.loop(0, chunks)
    def _(j):
        at = pl.ds(pl.multiple_of(j * chunk, chunk), chunk)
        load(j)[0].wait()
        block = caug[0:dim, at].astype(F32)
        hi, mid, lo = split3(-0.5 * jnp.sum(block * block, axis=0, keepdims=True))
        i = lax.broadcasted_iota(jnp.int32, (16, chunk), 0)
        extra = jnp.where(i == 3, hi, jnp.where(i == 4, mid, jnp.where(i == 5, lo, 0.0)))
        caug[dim : dim + 16, at] = jnp.where(i < 3, 1.0, extra).astype(BF16)
        caug[dim + 16 : DEPTH, at] = jnp.zeros((DEPTH - dim - 16, chunk), BF16)

    for j in range(chunks):
        load(j)[1].wait()
    total = jnp.zeros((rows, rank), F32)
    for s in range(cols // step):
        sat = slice(s * step, (s + 1) * step)
        kern = jnp.exp(dot(lhs, caug[:, sat], 1, 0) * scale).astype(BF16)
        total = total + dot(kern, panel[sat, :], 1, 0)
    part[...] = total.reshape(part.shape)

    pl.semaphore_wait(barrier, ncol + nrow - 2)

    for dz, dx in plane(nz, nx):
        to = col_at(dz, dx)
        put(RS, part.at[to], rs_buf.at[dz * nx + dx - 1], r, to)

    for dy in ring(ny):
        if dy:
            put(RPY, rp, rpb.at[y], row_at(dy, 0), c)
    rpb[y] = rp[...]

    landed(RS, rs_buf)
    total = part[c]
    for k in range(ncol - 1):
        total = total + rs_buf[k]
    srow[c] = total
    sy[y] = total
    for dy in ring(ny):
        if dy:
            put(SY, sy.at[y], sy.at[y], row_at(dy, 0), c)
    for dz, dx in plane(nz, nx):
        put(AGC, srow.at[c], srow.at[c], r, col_at(dz, dx))

    landed(SY, sy.at[pl.ds(0, ny - 1)])
    sg[x, z] = sy[...].reshape(ny * ch, rank).astype(BF16)
    for dz in ring(nz):
        if dz:
            put(stage_z(dz), sg.at[x, z], sg.at[x, z], r, col_at(dz, 0))

    landed(AGC, srow.at[pl.ds(0, ncol - 1)])
    sketch = srow[...].reshape(rows, rank)
    gpart[...] = dot(sketch.T, sketch, 1, 0, HIGH).reshape(gpart.shape)
    for dy, dc in plane(ny, 2):
        to = row_at(dy, dc)
        put(GRS, gpart.at[to], grs.at[dy * 2 + dc - 1], to, c)

    landed(RPY, rpb.at[pl.ds(0, ny - 1)])

    @pl.loop(0, ny)
    def _(j):
        t = aug_rows(rpb[j])
        for cc in range(ncol):
            rpt[cc % nx, cc // nx, j] = t[cc * ch : (cc + 1) * ch]

    sides = [1, nx - 1] if nx > 2 else [1]

    def forward(offsets):
        for dz in offsets:
            zz = lax.rem(z + dz, nz)
            for dx in ring(nx):
                if dx:
                    put(SX if dx in sides else SXF, sg.at[x, zz], sg.at[x, zz], r, col_at(0, dx))

    def partial(k):
        return dot(sg[k].reshape(deep, rank), k2[k], 0, 0)

    landed(SZ, sg.at[0, pl.ds(0, len(near_z))])
    forward([0] + near_z)

    deep = nz * ny * ch
    tile = min(512, deep)
    pair = 2 * own_cols

    @pl.loop(0, nx * (deep // tile))
    def _(j):
        jx, js = j // (deep // tile), lax.rem(j, deep // tile)
        zs = nz // (deep // tile)
        p = rpt[jx, pl.ds(js * zs, zs)].reshape(tile, DEPTH).astype(BF16)
        rat = pl.ds(pl.multiple_of(js * tile, tile), tile)
        for s in range(pair // step):
            sat = pl.ds(pl.multiple_of(y * pair + s * step, step), step)
            k2[jx, rat, s * step : (s + 1) * step] = jnp.exp(
                dot(p, caug[:, sat], 1, 0) * scale
            ).astype(BF16)

    landed(GRS, grs)
    gsum = gpart[r]
    for k in range(nrow - 1):
        gsum = gsum + grs[k]
    gfull[r] = gsum
    for dy, dc in plane(ny, 2):
        put(GAG, gfull.at[r], gfull.at[r], row_at(dy, dc), c)
    if far_z:
        landed(SZF, sg.at[0, pl.ds(0, len(far_z))])
        forward(far_z)
    tsum[...] = partial(x)
    landed(SX, sg.at[pl.ds(0, len(sides))])
    for dx in sides:
        tsum[...] += partial(lax.rem(x + dx, nx))
    if nx > 2:
        landed(SXF, sg.at[0])
    for k in (1 - core, core):
        half = pl.ds(pl.multiple_of(k * own_cols, own_cols), own_cols)
        t = tsum[:, half]
        if nx > 2:
            far = lax.rem(x + nx // 2, nx)
            t = t + dot(sg[far].reshape(deep, rank), k2[far, :, half], 0, 0)
        ts[k] = t
        if k is not core:
            for i in range(4):
                at = pl.ds(i * (rank // 4), rank // 4)
                put(TX, ts.at[1 - core, at], tr.at[at], partner, c)
    landed(GAG, gfull.at[pl.ds(0, nrow - 1)])

    inv = inverse_factor(gfull[...].reshape(rank, rank))
    hi, lo = split2(inv)
    inv_wide = jnp.concatenate([hi, hi, lo], axis=1)
    landed(TX, tr)
    hi, lo = split2(ts[core] + tr[...])
    coef = dot(inv_wide, jnp.concatenate([hi, lo, hi], axis=0), 1, 0).astype(BF16)
    for j in range(nrow):
        cs[j] = coef[j * gch : (j + 1) * gch]
    for dy, dc in plane(ny, 2):
        to = row_at(dy, dc)
        put(A2A, cs.at[to], cr.at[r], to, c)
    cr[r] = cs[r]
    left_ref[...] = dot(sketch, inv, 1, 1, HIGH) * math.sqrt(rows * nrow)

    left_us(RS, rs_buf)
    left_us(AGC, srow.at[pl.ds(0, ncol - 1)])
    left_us(SY, sy.at[pl.ds(0, ny - 1)])
    left_us(SZ, sg.at[0, pl.ds(0, len(near_z))])
    if far_z:
        left_us(SZF, sg.at[0, pl.ds(0, len(far_z))])
    left_us(SX, sg.at[pl.ds(0, len(sides))])
    if nx > 2:
        left_us(SXF, sg.at[0])
    left_us(RPY, rpb.at[pl.ds(0, ny - 1)])
    left_us(TX, tr)
    left_us(GRS, grs)
    left_us(GAG, gfull.at[pl.ds(0, nrow - 1)])
    landed(A2A, cr.at[pl.ds(0, nrow - 1)])
    for j in range(nrow):
        coef_ref[:, j * own_cols : (j + 1) * own_cols] = cr[j]
    left_us(A2A, cr.at[pl.ds(0, nrow - 1)])


def per_device(nrow, ncol, nx, row_points, col_points, random_panel):
    dim, rows = row_points.shape
    cols, rank = random_panel.shape
    nz, ny = ncol // nx, nrow // 2
    ch, gch, own_cols = rows // ncol, rank // nrow, cols // nrow
    chunk = min(1024, cols)
    vmem = pl.BlockSpec(memory_space=pltpu.VMEM)
    in_hbm = pl.BlockSpec(memory_space=pltpu.HBM)
    return pl.pallas_call(
        functools.partial(body, nrow, ncol, nx, chunk),
        out_shape=(
            jax.ShapeDtypeStruct((rows, rank), F32),
            jax.ShapeDtypeStruct((gch, cols), BF16),
        ),
        in_specs=[in_hbm] * 3,
        out_specs=(vmem, vmem),
        scratch_shapes=[
            pltpu.VMEM((dim, rows), BF16),
            pltpu.VMEM((DEPTH, cols), BF16),
            pltpu.VMEM((cols, rank), BF16),
            pltpu.VMEM((ncol, ch, rank), F32),
            pltpu.VMEM((ncol - 1, ch, rank), F32),
            pltpu.VMEM((ncol, ch, rank), F32),
            pltpu.VMEM((ny, ch, rank), F32),
            pltpu.VMEM((nx, nz, ny * ch, rank), BF16),
            pltpu.VMEM((ny, dim, rows), BF16),
            pltpu.VMEM((nx, nz, ny, ch, DEPTH), F32),
            pltpu.VMEM((nx, nz * ny * ch, 2 * own_cols), BF16),
            pltpu.VMEM((nrow, gch, rank), F32),
            pltpu.VMEM((nrow - 1, gch, rank), F32),
            pltpu.VMEM((nrow, gch, rank), F32),
            pltpu.VMEM((rank, 2 * own_cols), F32),
            pltpu.VMEM((2, rank, own_cols), F32),
            pltpu.VMEM((rank, own_cols), F32),
            pltpu.VMEM((nrow, gch, own_cols), BF16),
            pltpu.VMEM((nrow, gch, own_cols), BF16),
            pltpu.SemaphoreType.DMA((STAGES + 1,)),
            pltpu.SemaphoreType.DMA((STAGES + 1,)),
            pltpu.SemaphoreType.DMA((2, cols // chunk + 1)),
        ],
        compiler_params=pltpu.CompilerParams(
            collective_id=0, has_side_effects=True, vmem_limit_bytes=67043328 - 10900 * 1024
        ),
    )(*(pltpu.with_memory_space_constraint(v, pltpu.HBM) for v in (row_points, col_points, random_panel)))


def solution(mesh):
    nrow, ncol = mesh.shape["row"], mesh.shape["col"]
    nx = 4 if ncol % 8 == 0 else 2
    return jax.shard_map(
        functools.partial(per_device, nrow, ncol, nx),
        mesh=mesh,
        in_specs=(P(None, "row"), P(None, "col"), P("col", None)),
        out_specs=(P("row", None), P("row", "col")),
        check_vma=False,
    )
```

time: 395 us -> 50.4 us (0.13)
  waiting for transfers between devices: 324 us -> 0 us
  Pallas kernels: 0 us -> 48.3 us
  other arithmetic: 24 us -> 0 us
  matrix products: 20.4 us -> 0 us
  between operations: 13.8 us -> 0.64 us
  local copies, waits for them, and re-layouts: 10.6 us -> 1.31 us
    psum x2 -> x0, waiting for transfers between devices: 265 us -> none  [the longest x1 155 us: per_device(): sketch = lax.psum(partial_value, 'col')]
    unnamed x4 -> x0, waiting for transfers between devices: 59.4 us -> none
    pallas_call x0 -> x1, Pallas kernels: none -> 48.3 us  [per_device(): pl.pallas_call(functools.partial(body, nrow, ncol, nx, chunk), out_shape=...]
    another operation x5 -> x0, other arithmetic: 22.9 us -> none  [the longest x3 12.4 us: per_device(): factor = jnp.linalg.cholesky(gram_matrix)]
    dot_general x10 -> x0, matrix products: 18.6 us -> none  [the longest x4 6.73 us: kernel_tile(): jnp.einsum('kr,kc->rc', points_left, col_block, preferred_element_type=jn...]
    unnamed x6 -> x2, local copies, waits for them, and re-layouts: 5.32 us -> 1.31 us
  transfers between devices with their start and end apart: 3 -> 0, of which waited for: 3 -> 0; matrix products, arithmetic and copies ran while one was open for 0% -> 0% of each run, Pallas kernels for 0% -> 0%
where the time goes in v1:
time: 50.4 us; the launch traced here: 50.3 us
  Pallas kernels  48.3 us (96%)
  local copies, waits for them, and re-layouts  1.31 us (3%)
  between operations  0.64 us (1%)
    pallas_call x1, Pallas kernels, per_device(): pl.pallas_call(functools.partial(body, nrow, ncol, nx, chunk), out_shape=...  48.3 us
    unnamed x2, local copies, waits for them, and re-layouts  1.31 us

profile of v1, /device:TPU:1, one launch (start us, length us, event | category | flops | bytes accessed | tf_op | source)
XLA Modules:
  0.0 50.3 jit_solution(9706237427195864807)
XLA Ops:
  0.6 48.3 %shard_map.50 = (f32[256,128]{1,0:T(8,128)S(1)}, bf16[8,8192]{1,0:T(8,128)(2,1)S(1)}) custom-call(bf16[64,256]{1,0:T(8,128)(2,1)} %rp_hbm.1, bf16[64,8192]{1,0:T(8,128)(2,1)} %col_hbm.1, bf16[8192,128]{1,0:T(8,128)(2,1)} %panel_hbm.1), custom_call_target="tpu_custom_call" | custom-call | tf_op jit(solution)/shard_map/pallas_call | solution.py:346
  49.0 0.7 %copy.7 = f32[256,128]{1,0:T(8,128)} copy(f32[256,128]{1,0:T(8,128)S(1)} %get-tuple-element.4) | data formatting | bytes 262144
  49.6 0.7 %copy.8 = bf16[8,8192]{1,0:T(8,128)(2,1)} copy(bf16[8,8192]{1,0:T(8,128)(2,1)S(1)} %get-tuple-element.5) | data formatting | bytes 262144

commit v2 on v1

--- a/solution.py
+++ b/solution.py
@@ -56,9 +56,8 @@
         p = rows[b * tiles : (b + 1) * tiles]
         col = [None] * block
         diag = [None] * tiles
-        for i in range(block):
+        for i in range(0, block, 2):
             ti, si = i // 8, i % 8
-            at = lane == base + i
             stop = (i // inner + 1) * inner
             if i % inner == 0:
                 for j in range(i, stop):
@@ -67,34 +66,48 @@
                         jnp.broadcast_to(p[t][:, k : k + 1], (8, n)) if t >= j // 8 else None
                         for t in range(tiles)
                     ]
-            d = jnp.broadcast_to(col[i][ti][si : si + 1], (8, n))
-            diag[ti] = d if diag[ti] is None else jnp.where(sub == si, d, diag[ti])
-            inv = 1.0 / d
-            m = [None] * tiles
+
+            def at_row(v, k):
+                return jnp.broadcast_to(v[k : k + 1], (8, n))
+
+            c1, c2 = col[i], col[i + 1]
+            d1, e1, d2 = at_row(c1[ti], si), at_row(c1[ti], si + 1), at_row(c2[ti], si + 1)
+            det = d1 * d2 - e1 * e1
+            inv1, inv2 = 1.0 / d1, d1 * (1.0 / det)
+            diag[ti] = d1 if diag[ti] is None else jnp.where(sub == si, d1, diag[ti])
+            diag[ti] = jnp.where(sub == si + 1, det * inv1, diag[ti])
+            m1, m2 = [None] * tiles, [None] * tiles
             for t in range(ti, tiles):
-                m[t] = col[i][t] * inv
-            m[ti] = jnp.where(sub > si, m[ti], 0.0)
-            for j in range(i + 1, stop):
-                e = jnp.broadcast_to(col[i][j // 8][j % 8 : j % 8 + 1], (8, n))
+                m1[t] = c1[t] * inv1
+                if t == ti:
+                    m1[t] = jnp.where(sub > si, m1[t], 0.0)
+                c2[t] = c2[t] - m1[t] * e1
+                m2[t] = c2[t] * inv2
+                if t == ti:
+                    m2[t] = jnp.where(sub > si + 1, m2[t], 0.0)
+            for j in range(i + 2, stop):
+                f1, f2 = at_row(c1[j // 8], j % 8), at_row(c2[j // 8], j % 8)
                 for t in range(j // 8, tiles):
-                    col[j][t] = col[j][t] - m[t] * e
-            row = jnp.where(at, 1.0, jnp.broadcast_to(p[ti][si : si + 1], (8, n)))
-            for t in range(ti, tiles):
-                keep = (sub == si).astype(F32) if t == ti else 0.0
-                p[t] = jnp.where(at, keep, p[t]) - m[t] * row
+                    col[j][t] = col[j][t] - m1[t] * f1 - m2[t] * f2
+            for m, s in ((m1, si), (m2, si + 1)):
+                at = lane == base + 8 * ti + s
+                row = jnp.where(at, 1.0, at_row(p[ti], s))
+                for t in range(ti, tiles):
+                    keep = (sub == s).astype(F32) if t == ti else 0.0
+                    p[t] = jnp.where(at, keep, p[t]) - m[t] * row
         for t in range(tiles):
             dead = (lane > sub + (base + 8 * t)) & (lane < base + block)
             p[t] = jnp.where(dead, 0.0, p[t] * lax.rsqrt(diag[t]))
             rows[b * tiles + t] = p[t]
         if b + 1 < count:
-            panel = jnp.concatenate(p, axis=0)
-            turned = panel.T
+            hi, mid, lo = (v.astype(BF16) for v in split3(jnp.concatenate(p, axis=0)))
+            stacked = jnp.concatenate([hi, hi, hi, mid, mid, lo], axis=0)
+            upd = dot(stacked, jnp.concatenate([hi, mid, lo, hi, mid, hi], axis=0), 0, 0)
             inside = (lane >= base) & (lane < base + block)
             for u in range(b + 1, count):
-                upd = dot(turned[u * block : (u + 1) * block], panel, 1, 0, HIGH)
                 for t in range(tiles):
                     at = u * tiles + t
-                    rows[at] = jnp.where(inside, 0.0, rows[at]) - upd[8 * t : 8 * t + 8]
+                    rows[at] = jnp.where(inside, 0.0, rows[at]) - upd[8 * at : 8 * at + 8]
     rows = [jnp.where(lane > sub + 8 * t, 0.0, rows[t]) for t in range(n // 8)]
     return jnp.concatenate(rows, axis=0)
 
@@ -273,6 +286,9 @@
                 dot(p, caug[:, sat], 1, 0) * scale
             ).astype(BF16)
 
+    if far_z:
+        landed(SZF, sg.at[0, pl.ds(0, len(far_z))])
+        forward(far_z)
     landed(GRS, grs)
     gsum = gpart[r]
     for k in range(nrow - 1):
@@ -280,9 +296,6 @@
     gfull[r] = gsum
     for dy, dc in plane(ny, 2):
         put(GAG, gfull.at[r], gfull.at[r], row_at(dy, dc), c)
-    if far_z:
-        landed(SZF, sg.at[0, pl.ds(0, len(far_z))])
-        forward(far_z)
     tsum[...] = partial(x)
     landed(SX, sg.at[pl.ds(0, len(sides))])
     for dx in sides:
@@ -335,6 +348,17 @@
     left_us(A2A, cr.at[pl.ds(0, nrow - 1)])
 
 
+def hand_out(left_in, coef_in, left_out, coef_out, sem):
+    copies = [
+        pltpu.make_async_copy(left_in, left_out, sem.at[0]),
+        pltpu.make_async_copy(coef_in, coef_out, sem.at[1]),
+    ]
+    for copy in copies:
+        copy.start()
+    for copy in copies:
+        copy.wait()
+
+
 def per_device(nrow, ncol, nx, row_points, col_points, random_panel):
     dim, rows = row_points.shape
     cols, rank = random_panel.shape
@@ -343,7 +367,8 @@
     chunk = min(1024, cols)
     vmem = pl.BlockSpec(memory_space=pltpu.VMEM)
     in_hbm = pl.BlockSpec(memory_space=pltpu.HBM)
-    return pl.pallas_call(
+    out_hbm = pl.BlockSpec(memory_space=pltpu.HBM)
+    found = pl.pallas_call(
         functools.partial(body, nrow, ncol, nx, chunk),
         out_shape=(
             jax.ShapeDtypeStruct((rows, rank), F32),
@@ -378,7 +403,20 @@
         compiler_params=pltpu.CompilerParams(
             collective_id=0, has_side_effects=True, vmem_limit_bytes=67043328 - 10900 * 1024
         ),
-    )(*(pltpu.with_memory_space_constraint(v, pltpu.HBM) for v in (row_points, col_points, random_panel)))
+    )(
+        *(
+            pltpu.with_memory_space_constraint(v, pltpu.HBM)
+            for v in (row_points, col_points, random_panel)
+        )
+    )
+    return pl.pallas_call(
+        hand_out,
+        out_shape=tuple(jax.ShapeDtypeStruct(v.shape, v.dtype) for v in found),
+        in_specs=[pl.BlockSpec(memory_space=pl.ANY)] * 2,
+        out_specs=(out_hbm, out_hbm),
+        scratch_shapes=[pltpu.SemaphoreType.DMA((2,))],
+        compiler_params=pltpu.CompilerParams(vmem_limit_bytes=1024 * 1024),
+    )(*found)
 
 
 def solution(mesh):

time: 50.4 us -> 49.4 us (0.980)
  local copies, waits for them, and re-layouts: 1.31 us -> 0 us
    unnamed x2 -> x0, local copies, waits for them, and re-layouts: 1.31 us -> none
    pallas_call x0 -> x1, Pallas kernels: none -> 0.72 us  [per_device(): pl.pallas_call(hand_out, out_shape=tuple((jax.ShapeDtypeStruct(v.shape, v...]
where the time goes in v2:
time: 49.4 us; the launch traced here: 49.2 us
  Pallas kernels  48.6 us (98%)
  between operations  0.64 us (1%)
    pallas_call x1, Pallas kernels, per_device(): pl.pallas_call(functools.partial(body, nrow, ncol, nx, chunk), out_shape=...  47.9 us

profile of v2, /device:TPU:1, one launch (start us, length us, event | category | flops | bytes accessed | tf_op | source)
XLA Modules:
  0.0 49.2 jit_solution(17953314516869592626)
XLA Ops:
  0.6 47.9 %shard_map.50 = (f32[256,128]{1,0:T(8,128)S(1)}, bf16[8,8192]{1,0:T(8,128)(2,1)S(1)}) custom-call(bf16[64,256]{1,0:T(8,128)(2,1)} %rp_hbm.1, bf16[64,8192]{1,0:T(8,128)(2,1)} %col_hbm.1, bf16[8192,128]{1,0:T(8,128)(2,1)} %panel_hbm.1), custom_call_target="tpu_custom_call" | custom-call | tf_op jit(solution)/shard_map/pallas_call | solution.py:371
  48.5 0.7 %shard_map.51 = (f32[256,128]{1,0:T(8,128)}, bf16[8,8192]{1,0:T(8,128)(2,1)}) custom-call(f32[256,128]{1,0:T(8,128)S(1)} %get-tuple-element.4.left_in, bf16[8,8192]{1,0:T(8,128)(2,1)S(1)} %get-tuple-element.5.coef_in), custom_call_target="tpu_custom_call" | custom-call | tf_op jit(solution)/shard_map/pallas_call | solution.py:412
